TPU v7x, 128 devices: a whole 4x4x4 slice. The times are simulated.
128 devices in a mesh: obs: 8 (over z_lo, y), tm: 16 (over x, z_hi, core).
Axes of the slice: x: 4, y: 4, z: 4 (z_hi: 2, z_lo: 2; z = z_hi * 2 + z_lo), core: 2. Of those that a mesh axis runs over, the one named last changes fastest.
Arguments:
- footprints: bfloat16 [4096, 16, 2048], P('obs', 'tm'), may hold values from -0.125 to 0.125
- spatial_cov: bfloat16 [2048, 2048], replicated, may hold values from -2 to 11, as said below
- time_cov: float32 [16, 16], replicated, may hold values from -1 to 3, as said below
- flux_draws: bfloat16 [256, 16, 2048], P('obs', 'tm'), may hold values from -6 to 6
- perturbed: float32 [4096, 256], P('obs'), may hold values from -96 to 96
- obs_error: float32 [4096], P('obs'), may hold values from 16 to 64
Outputs:
- weights: float32 [4096, 256], P(('obs', 'tm'))
- update: float32 [256, 16, 2048], P('obs', 'tm')
Inputs may be any that keep to these rules, and one draw needn't show every extreme that they name: `spatial_cov`: symmetric. `time_cov`: symmetric.
All inputs are finite; a program needn't handle non-finite values.
Results may differ from a plain program's by a relative error of at most 0.0059.
Values may be sent and summed in bfloat16 or wider, within the bound.
A program may use at most 128 MiB of HBM per device.

v0:
```python
import jax
import jax.numpy as jnp
from jax import lax
from jax.sharding import PartitionSpec as P

SWEEPS = 2


def joined_along(parts, dim):
    shape = list(parts.shape[1:])
    shape[dim] *= parts.shape[0]
    return jnp.moveaxis(parts, 0, dim).reshape(shape)


def copy_for_each(value, axis):
    size = lax.axis_size(axis)
    return lax.all_to_all(
        jnp.broadcast_to(value[None], (size, *value.shape)), axis, 0, 0, tiled=True
    )


def gather_directly(value, axis, dim):
    return joined_along(copy_for_each(value, axis), dim)


def cut_along(value, dim, size):
    before, after = (value.shape[:dim], value.shape[dim + 1 :])
    return jnp.moveaxis(value.reshape(*before, size, -1, *after), dim, 0)


def summed_on_arrival(value, axis, dim):
    parts = cut_along(value, dim, lax.axis_size(axis))
    arrived = lax.all_to_all(parts, axis, split_axis=0, concat_axis=0, tiled=True)
    return arrived.sum(axis=0)


def contract_last(left, right):
    return lax.dot_general(
        left, right, (((1,), (1,)), ((), ())), preferred_element_type=jnp.float32
    )


def body(footprints, spatial_cov, time_cov, flux_draws, perturbed, obs_error):
    rows_obs = footprints.shape[0]
    period = lax.axis_index("tm")
    obs_group = lax.axis_index("obs")
    own_rows = footprints[:, 0, :]
    spread = jnp.dot(own_rows, spatial_cov, preferred_element_type=jnp.float32).astype(jnp.bfloat16)
    mixing = jnp.einsum(
        "ntc,ts->nsc",
        lax.all_to_all(spread[:, None, :], "tm", split_axis=2, concat_axis=1, tiled=True).astype(
            jnp.float32
        ),
        time_cov,
        precision=lax.Precision.HIGHEST,
    ).astype(jnp.bfloat16)
    mixed = lax.all_to_all(mixing, "tm", split_axis=1, concat_axis=2, tiled=True)[:, 0, :]
    draw_rows = gather_directly(flux_draws[:, 0, :], "obs", 0)
    all_footprints = lax.all_gather(own_rows, "obs", axis=0, tiled=True)
    total_obs = all_footprints.shape[0]
    row_share = rows_obs // lax.axis_size("tm")
    summed = lax.psum(
        jnp.concatenate(
            [contract_last(mixed, all_footprints), contract_last(own_rows, draw_rows)], axis=1
        ),
        "tm",
    )
    covariance = summed[:, :total_obs]
    predicted = summed[:, total_obs:]
    square = lax.dynamic_slice_in_dim(covariance, obs_group * rows_obs, rows_obs, 1)
    divisor = jnp.diagonal(square) + obs_error
    residual = perturbed - predicted
    weights = residual / divisor[:, None]
    for sweep_index in range(SWEEPS):
        gathered = lax.all_gather(weights, "obs", axis=0, tiled=True)
        product = jnp.dot(covariance, gathered, precision=lax.Precision.HIGHEST)
        weights = weights + (residual - product - obs_error[:, None] * weights) / divisor[:, None]
    out_weights = lax.dynamic_slice_in_dim(weights, period * row_share, row_share, 0)
    rounded = weights.astype(jnp.bfloat16)
    update = summed_on_arrival(
        lax.dot_general(
            rounded, mixed, (((0,), (0,)), ((), ())), preferred_element_type=jnp.float32
        ),
        "obs",
        0,
    )
    return (out_weights, update[:, None, :])


def solution(mesh):
    in_specs = (P("obs", "tm", None), P(), P(), P("obs", "tm", None), P("obs", None), P("obs"))
    out_specs = (P(("obs", "tm"), None), P("obs", "tm", None))
    return jax.shard_map(body, mesh=mesh, in_specs=in_specs, out_specs=out_specs, check_vma=False)
```

profile of v0, /device:TPU:1, one launch (start us, length us, event | category | flops | bytes accessed | tf_op | source)
XLA Modules:
  0.0 675.4 jit_solution(17676830024850842765)
XLA Ops:
  7.9 8.5 %fusion.2 = bf16[512,1,2048]{2,0,1:T(8,128)(2,1)S(1)} fusion(bf16[2048,2048]{1,0:T(8,128)(2,1)} %param.7, bf16[512,1,2048]{2,0,1:T(8,128)(2,1)} %param.6), kind=kOutput, calls=%fused_computation.5 | convolution fusion | flops 4296015872 | bytes 12582912 | tf_op jit(solution)/shard_map/dot_general | solution.py:48
  16.4 7.5 %copy.14 = bf16[512,1,2048]{0,1,2:T(2,128)(2,1)} copy(bf16[512,1,2048]{2,0,1:T(8,128)(2,1)S(1)} %fusion.2) | data formatting | bytes 4194304 | tf_op jit(solution)/shard_map/broadcast_in_dim | solution.py:51
  24.5 14.1 %reduce = bf16[2048,512]{1,0:T(8,128)(2,1)S(1)} reduce(bf16[2048,1,512]{2,1,0:T(2,128)(2,1)} %bitcast.39, bf16[]{:T(256)} %broadcast.23), dimensions={1}, to_apply=%bitcast.26.reduce_sub_computation | reduce | bytes 4194306
  41.4 165.8 %all_to_all.31 = bf16[16,2,32768]{2,1,0:T(2,128)(2,1)S(1)} all-to-all(bf16[16,2,32768]{2,1,0:T(2,128)(2,1)} %reshape.31), channel_id=1, replica_groups=mesh['obs'=8,'tm'=16] {'tm'}, dimensions={0} | all-to-all | bytes 4194304 | tf_op jit(solution)/shard_map/all_to_all | solution.py:51
  208.3 3.6 all-to-all-start.2
  211.9 6.7 reshape.32
  224.5 3.4 convert_bitcast_fusion
  229.8 4.7 all-to-all-start.1
  234.7 3.1 fusion.5
  237.9 25.1 %all-to-all-done.1 = bf16[512,16,128]{2,0,1:T(8,128)(2,1)S(1)} async-done(((bf16[512,16,128]{2,0,1:T(8,128)(2,1)}), bf16[512,16,128]{2,0,1:T(8,128)(2,1)S(1)}, u32[]{:S(2)}, u32[]{:S(2)}) %all-to-all-start.1) | async-done | bytes 2097184 | tf_op jit(solution)/shard_map/all_to_all | solution.py:57
  263.0 15.4 %fusion = f32[512,4096]{1,0:T(8,128)} fusion(bf16[4096,1,2048]{2,0,1:T(8,128)(2,1)} %all-gather.9.cloned.1.call-done, bf16[512,16,128]{2,0,1:T(8,128)(2,1)S(1)} %all-to-all-done.1), kind=kOutput, calls=%fused_computation.1 | convolution fusion | flops 8589934592 | bytes 27262976 | tf_op jit(solution)/shard_map/dot_general | solution.py:38
  278.4 7.5 %pad_maximum_fusion = f32[512,4352]{1,0:T(8,128)} fusion(f32[512,256]{1,0:T(8,128)S(1)} %copy-done.5, f32[512,4096]{1,0:T(8,128)} %fusion), kind=kLoop, calls=%fused_computation.3 | loop fusion | flops 2228224 | bytes 17825792 | tf_op jit(solution)/shard_map/concatenate | solution.py:63
  286.0 211.0 %all-reduce.2.cloned.1.call-done = f32[512,4352]{1,0:T(8,128)} async-done(((f32[512,4352]{1,0:T(8,128)}), f32[512,4352]{1,0:T(8,128)}) %all-reduce.2.cloned.1.call-update) | async-done | bytes 8912912 | tf_op jit(solution)/shard_map/psum | solution.py:62
  497.0 3.4 slice-done
  500.5 4.5 gather_fusion
  507.1 52.1 %all-gather.5.cloned.1.call-done = f32[4096,256]{1,0:T(8,128)} async-done(((f32[512,256]{1,0:T(8,128)}), f32[4096,256]{1,0:T(8,128)}) %all-gather.5.cloned.1.call-update) | async-done | bytes 4194320 | tf_op jit(solution)/shard_map/all_gather | solution.py:75
  559.3 11.6 %fusion.11 = f32[512,256]{1,0:T(8,128)} fusion(f32[4096,256]{1,0:T(8,128)} %all-gather.5.cloned.1.call-done, f32[512]{0:T(512)S(1)} %copy-done.6, f32[512]{0:T(512)S(1)} %add.22, f32[512,256]{1,0:T(8,128)S(1)} %copy-done.2, f32[512,4352]{1,0:T(8,128)} %all-reduce.2.cloned.1.call-done), kind=kOutput, calls=%fused_computation.17 | convolution fusion | flops 6443368448 | bytes 14159872 | tf_op jit(solution)/shard_map/dot_general | solution.py:76
  570.9 4.3 copy.18
  575.2 4.2 reshape.28
  579.3 43.1 %all-gather.7.cloned.1.call-done = f32[4096,256]{1,0:T(8,128)} async-done(((f32[512,256]{1,0:T(8,128)}), f32[4096,256]{1,0:T(8,128)}) %all-gather.7.cloned.1.call-update) | async-done | bytes 4194320 | tf_op jit(solution)/shard_map/all_gather | solution.py:75
  622.4 10.9 %fusion.13 = f32[512,256]{1,0:T(8,128)S(1)} fusion(f32[512,256]{1,0:T(8,128)S(1)} %copy-done.3, f32[4096,256]{1,0:T(8,128)} %all-gather.7.cloned.1.call-done, f32[512]{0:T(512)S(1)} %copy-done.6, f32[512]{0:T(512)S(1)} %add.22, f32[512,256]{1,0:T(8,128)S(1)} %copy-done.2, f32[512,4352]{1,0:T(8,128)} %all-reduce.2.cloned.1.call-done), kind=kOutput, calls=%fused_computation.19 | convolution fusion | flops 6443237376 | bytes 14684160 | tf_op jit(solution)/shard_map/dot_general | solution.py:76
  633.5 3.7 fusion.17
  637.2 3.6 all-to-all-start.3
  641.4 26.4 %all-to-all-done.3 = f32[8,32,2048]{2,1,0:T(8,128)S(1)} async-done(((f32[8,32,2048]{2,1,0:T(8,128)}), f32[8,32,2048]{2,1,0:T(8,128)S(1)}, u32[]{:S(2)}, u32[]{:S(2)}) %all-to-all-start.3) | async-done | bytes 2097184 | tf_op jit(solution)/shard_map/all_to_all | solution.py:33
  (42 shorter events, 17.2 us)
Async XLA Ops:
  7.2 217.3 %copy-start = (f32[16,16]{1,0:T(8,128)S(1)}, f32[16,16]{1,0:T(8,128)}, u32[]{:S(2)}) copy-start(f32[16,16]{1,0:T(8,128)} %param.8) | copy-start | bytes 3076
  7.2 255.8 %all-gather.9.cloned.1.call-start = ((), (), s32[]{:S(2)}) async-start(), calls=%async_computation.7 | async-start | bytes 18874368 | tf_op jit(solution)/shard_map/all_gather | solution.py:59
  38.6 168.6 %copy-start.7 = (bf16[32,1,2048]{2,0,1:T(8,128)(2,1)S(1)}, bf16[32,1,2048]{2,0,1:T(8,128)(2,1)}, u32[]{:S(2)}) copy-start(bf16[32,1,2048]{2,0,1:T(8,128)(2,1)} %param.9) | copy-start | bytes 393220
  208.3 21.5 %all-to-all-start.2 = ((bf16[8,32,2048]{2,1,0:T(8,128)(2,1)}), bf16[8,32,2048]{2,1,0:T(8,128)(2,1)S(1)}, u32[]{:S(2)}, u32[]{:S(2)}) async-start(bf16[8,32,2048]{2,1,0:T(8,128)(2,1)} %broadcast_in_dim.24), calls=%async_computation.2 | async-start | bytes 2097152 | tf_op jit(solution)/shard_map/all_to_all | solution.py:17
  229.8 33.1 %all-to-all-start.1 = ((bf16[512,16,128]{2,0,1:T(8,128)(2,1)}), bf16[512,16,128]{2,0,1:T(8,128)(2,1)S(1)}, u32[]{:S(2)}, u32[]{:S(2)}) async-start(bf16[512,16,128]{2,0,1:T(8,128)(2,1)} %copy.17), calls=%async_computation.1 | async-start | bytes 4194304 | tf_op jit(solution)/shard_map/all_to_all | solution.py:57
  234.5 262.5 %all-reduce.2.cloned.1.call-start = ((), (), s32[]{:S(2)}) async-start(), calls=%async_computation.4 | async-start | bytes 17825792 | tf_op jit(solution)/shard_map/psum | solution.py:62
  237.9 40.5 %copy-start.5 = (f32[512,256]{1,0:T(8,128)S(1)}, f32[512,256]{1,0:T(8,128)}, u32[]{:S(2)}) copy-start(f32[512,256]{1,0:T(8,128)} %fusion.5) | copy-start | bytes 1572868
  263.0 15.4 %copy-start.4 = (bf16[512,16,128]{2,0,1:T(8,128)(2,1)}, bf16[512,16,128]{2,0,1:T(8,128)(2,1)S(1)}, u32[]{:S(2)}) copy-start(bf16[512,16,128]{2,0,1:T(8,128)(2,1)S(1)} %all-to-all-done.1) | copy-start | bytes 6291460
  285.9 273.3 %all-gather.5.cloned.1.call-start = ((), (), s32[]{:S(2)}) async-start(), calls=%async_computation.5 | async-start | bytes 4718592 | tf_op jit(solution)/shard_map/all_gather | solution.py:75
  497.0 3.4 slice-start
  500.4 4.6 copy-start.6
  500.4 4.7 copy-start.2
  507.1 115.3 %all-gather.7.cloned.1.call-start = ((), (), s32[]{:S(2)}) async-start(), calls=%async_computation.6 | async-start | bytes 4718592 | tf_op jit(solution)/shard_map/all_gather | solution.py:75
  570.9 51.5 %copy-start.3 = (f32[512,256]{1,0:T(8,128)S(1)}, f32[512,256]{1,0:T(8,128)}, u32[]{:S(2)}) copy-start(f32[512,256]{1,0:T(8,128)} %fusion.11) | copy-start | bytes 1572868
  633.5 35.3 %copy-start.1 = (f32[16,16]{1,0:T(8,128)S(1)}, f32[16,16]{1,0:T(8,128)}, u32[]{:S(2)}) copy-start(f32[16,16]{1,0:T(8,128)} %param.8) | copy-start | bytes 3076
  637.2 30.6 %all-to-all-start.3 = ((f32[8,32,2048]{2,1,0:T(8,128)}), f32[8,32,2048]{2,1,0:T(8,128)S(1)}, u32[]{:S(2)}, u32[]{:S(2)}) async-start(f32[8,32,2048]{2,1,0:T(8,128)} %fusion.17), calls=%async_computation.3 | async-start | bytes 4194304 | tf_op jit(solution)/shard_map/all_to_all | solution.py:33
Sparse Core Ops, SparseCore 0:
  9.7 190.7 all-gather.8
  286.0 210.9 all-reduce.1
  507.2 51.9 all-gather.4
  571.0 51.3 all-gather.6
where the time goes:
time: 677 us; the launch traced here: 675 us
  waiting for transfers between devices  358 us (53%)
  blocking collectives  166 us (25%)
  matrix products  56.7 us (8%)
  local copies, waits for them, and re-layouts  44.6 us (7%)
  other arithmetic  23.8 us (4%)
  between operations  13.9 us (2%)
  starting transfers between devices  12.2 us (2%)
    psum x1, waiting for transfers between devices, body(): lax.psum(jnp.concatenate([contract_last(mixed, all_footprints), contract_...  211 us
    all_to_all x1, blocking collectives, body(): lax.all_to_all(spread[:, None, :], 'tm', split_axis=2, concat_axis=1, til...  166 us
    all_gather x2, waiting for transfers between devices, body(): gathered = lax.all_gather(weights, 'obs', axis=0, tiled=True)  95.2 us
    all_to_all x1, waiting for transfers between devices, summed_on_arrival(): lax.all_to_all(parts, axis, split_axis=0, concat_axis=0, tiled=True)  26.4 us
    all_to_all x1, waiting for transfers between devices, body(): lax.all_to_all(mixing, 'tm', split_axis=1, concat_axis=2, tiled=True)  25.1 us
    dot_general x2, matrix products, body(): product = jnp.dot(covariance, gathered, precision=lax.Precision.HIGHEST)  22.5 us
    dot_general x2, matrix products, contract_last(): lax.dot_general(left, right, (((1,), (1,)), ((), ())), preferred_element_...  18.5 us
    unnamed x1, other arithmetic  14.1 us
  transfers between devices with their start and end apart: 7, of which 5 were waited for; matrix products, arithmetic and copies ran while one was open for 10% of the time, Pallas kernels for 0%

commit v1 on v0

v1 whole, which is shorter than its diff:
```python
import functools

import jax
import jax.numpy as jnp
from jax import lax
from jax.experimental import pallas as pl
from jax.experimental.pallas import tpu as pltpu
from jax.sharding import PartitionSpec as P

SWEEPS = 2
MESH = pl.DeviceIdType.MESH
BF16 = jnp.bfloat16
F32 = jnp.float32
TILE = 256
BATCHES = 4


def dot_nt(left, right):
    return lax.dot_general(left, right, (((1,), (1,)), ((), ())), preferred_element_type=F32)


def dot_nn(left, right):
    return jnp.dot(left, right, preferred_element_type=F32)


def rows_at(start, size):
    return pl.ds(pl.multiple_of(start, size), size)


def kernel(
    n_obs, n_tm,
    f_ref, s_ref, t_ref, d_ref, p_ref, e_ref,
    w_ref, u_ref,
    f_v, s_v, frow, spread, mrow, mixed, dall, psend, prow,
    wall, wt, gp, grs, gall, ysend, yrow, k_hi, k_lo, pert, dacc,
    local_sem, send_sem, recv_sem, frecv_sem,
):
    o = lax.axis_index("obs")
    t = lax.axis_index("tm")
    rows, cells = f_ref.shape
    share = rows // n_tm
    draws = d_ref.shape[0]
    per_batch = n_tm // BATCHES

    def tm_peer(r):
        return lax.rem(t + r, n_tm)

    def tm_source(r):
        return lax.rem(t - r + n_tm, n_tm)

    def obs_peer(q):
        return lax.rem(o + q, n_obs)

    def send(src, dst, phase, axis, peer, recv=None):
        pltpu.make_async_remote_copy(
            src_ref=src, dst_ref=dst, send_sem=send_sem.at[phase],
            recv_sem=recv_sem.at[phase] if recv is None else recv,
            device_id={axis: peer}, device_id_type=MESH,
        ).start()

    def await_bytes(region, sem):
        pltpu.make_async_copy(region, region, sem).wait()

    load_s = pltpu.make_async_copy(s_ref, s_v, local_sem.at[0])
    load_f = pltpu.make_async_copy(f_ref, f_v, local_sem.at[1])
    load_p = pltpu.make_async_copy(p_ref.at[rows_at(t * share, share)], pert, local_sem.at[2])
    own_f = pltpu.make_async_copy(f_ref.at[rows_at(t * share, share)], frow.at[pl.ds(0, share)], local_sem.at[3])
    own_d = pltpu.make_async_copy(d_ref, dall.at[rows_at(o * draws, draws)], local_sem.at[4])

    barrier = pltpu.get_barrier_semaphore()

    @pl.loop(1, n_tm)
    def _(r):
        pl.semaphore_signal(barrier, inc=1, device_id={"tm": tm_peer(r)}, device_id_type=MESH)

    @pl.loop(1, n_obs)
    def _(q):
        pl.semaphore_signal(barrier, inc=1, device_id={"obs": obs_peer(q)}, device_id_type=MESH)

    load_f.start()
    own_f.start()
    own_d.start()
    load_p.start()
    load_s.start()
    pl.semaphore_wait(barrier, n_tm - 1 + n_obs - 1)

    @pl.loop(1, n_obs)
    def _(q):
        send(d_ref, dall.at[rows_at(o * draws, draws)], 0, "obs", obs_peer(q))

    @pl.loop(1, n_tm)
    def _(r):
        peer = tm_peer(r)
        send(
            f_ref.at[rows_at(peer * share, share)], frow.at[rows_at(r * share, share)],
            1, "tm", peer, frecv_sem.at[r // per_batch],
        )

    ids = lax.broadcasted_iota(jnp.int32, (rows, n_tm), 0) // share
    pick = (lax.rem(t - ids + n_tm, n_tm) == lax.broadcasted_iota(jnp.int32, (rows, n_tm), 1)).astype(F32)
    ids_t = lax.broadcasted_iota(jnp.int32, (n_tm, rows), 1) // share
    pick_t = (lax.rem(t - ids_t + n_tm, n_tm) == lax.broadcasted_iota(jnp.int32, (n_tm, rows), 0)).astype(F32)
    picked = jnp.dot(t_ref[...], pick_t, precision=lax.Precision.HIGHEST, preferred_element_type=F32)
    full = jnp.dot(pick, picked, precision=lax.Precision.HIGHEST, preferred_element_type=F32)
    row_in = lax.rem(lax.broadcasted_iota(jnp.int32, (rows, rows), 0), share)
    col_in = lax.rem(lax.broadcasted_iota(jnp.int32, (rows, rows), 1), share)
    full = jnp.where(row_in == col_in, full, 0.0)
    high = full.astype(BF16)
    k_hi[...] = high
    k_lo[...] = (full - high.astype(F32)).astype(BF16)

    load_f.wait()
    own_d.wait()
    await_bytes(dall.at[pl.ds(0, (n_obs - 1) * draws)], recv_sem.at[0])
    psend[...] = dot_nt(f_v[...], dall[...])

    @pl.loop(1, n_tm)
    def _(r):
        peer = tm_peer(r)
        send(psend.at[rows_at(peer * share, share)], prow.at[rows_at(r * share, share)], 2, "tm", peer)

    own_f.wait()
    load_s.wait()
    size = per_batch * share
    for batch in range(BATCHES):
        first = share if batch == 0 else 0
        await_bytes(frow.at[pl.ds(batch * size + first, size - first)], frecv_sem.at[batch])

        @pl.loop(0, cells // TILE)
        def _(c):
            cols = pl.ds(pl.multiple_of(c * TILE, TILE), TILE)
            here = pl.ds(batch * size, size)
            spread[here, cols] = dot_nn(frow[here, :], s_v[:, cols]).astype(BF16)

    dacc[...] = jnp.zeros_like(dacc)

    @pl.loop(0, cells // TILE)
    def _(c):
        cols = pl.ds(pl.multiple_of(c * TILE, TILE), TILE)
        block = spread[:, cols]
        out = (dot_nn(k_hi[...], block) + dot_nn(k_lo[...], block)).astype(BF16)
        mrow[:, cols] = out
        product = out.astype(F32) * frow[:, cols].astype(F32)
        dacc[...] += product.reshape(n_tm, share, TILE).sum(axis=0)

    load_p.wait()
    await_bytes(prow.at[pl.ds(share, rows - share)], recv_sem.at[2])
    predicted = psend[rows_at(t * share, share), :]
    predicted += prow[pl.ds(share, rows - share), :].reshape(n_tm - 1, share, -1).sum(axis=0)
    residual = pert[...] - predicted
    at_row = lax.broadcasted_iota(jnp.int32, (share, rows), 0) + t * share
    at_col = lax.broadcasted_iota(jnp.int32, (share, rows), 1)
    error = jnp.where(at_row == at_col, jnp.broadcast_to(e_ref[...], (share, rows)), 0.0).sum(axis=1, keepdims=True)
    divisor = dacc[...].sum(axis=1, keepdims=True) + error

    def share_weights(step, weights):
        wall[step, rows_at(t * share, share), :] = weights.astype(BF16)

        @pl.loop(1, n_tm)
        def _(r):
            here = wall.at[step, rows_at(t * share, share)]
            send(here, here, 4 + step, "tm", tm_peer(r))

    def weighted(step, matrix):
        await_bytes(wall.at[step, pl.ds(share, rows - share)], recv_sem.at[4 + step])
        wt[...] = wall[step].T

        @pl.loop(0, cells // TILE)
        def _(c):
            cols = pl.ds(pl.multiple_of(c * TILE, TILE), TILE)
            gp[step, :, cols] = dot_nn(wt[...], matrix[:, cols]).astype(BF16)

        @pl.loop(1, n_obs)
        def _(q):
            peer = obs_peer(q)
            send(
                gp.at[step, rows_at(peer * draws, draws)], grs.at[step, rows_at(q * draws, draws)],
                7 + step, "obs", peer,
            )

        await_bytes(grs.at[step, pl.ds(draws, (n_obs - 1) * draws)], recv_sem.at[7 + step])
        total = gp[step, rows_at(o * draws, draws), :].astype(F32)
        for q in range(1, n_obs):
            total += grs[step, pl.ds(q * draws, draws), :].astype(F32)
        return total

    weights = residual / divisor
    share_weights(0, weights)
    own_m = pltpu.make_async_copy(mrow.at[pl.ds(0, share)], mixed.at[rows_at(t * share, share)], local_sem.at[5])
    own_m.start()

    @pl.loop(1, n_tm)
    def _(r):
        send(mrow.at[rows_at(r * share, share)], mixed.at[rows_at(t * share, share)], 3, "tm", tm_source(r))

    for step in range(SWEEPS):
        total = weighted(step, f_v)
        here = gall.at[step, rows_at(o * draws, draws)]
        gall[step, rows_at(o * draws, draws), :] = total.astype(BF16)

        @pl.loop(1, n_obs)
        def _(q):
            send(here, here, 10 + step, "obs", obs_peer(q))

        if step == 0:
            own_m.wait()
            await_bytes(mixed.at[pl.ds(share, rows - share)], recv_sem.at[3])
        await_bytes(gall.at[step, pl.ds(draws, (n_obs - 1) * draws)], recv_sem.at[10 + step])
        ysend[step] = dot_nt(mixed[...], gall[step]).astype(BF16)

        @pl.loop(1, n_tm)
        def _(r):
            peer = tm_peer(r)
            send(
                ysend.at[step, rows_at(peer * share, share)], yrow.at[step, rows_at(r * share, share)],
                12 + step, "tm", peer,
            )

        await_bytes(yrow.at[step, pl.ds(share, rows - share)], recv_sem.at[12 + step])
        product = ysend[step, rows_at(t * share, share), :].astype(F32)
        product += yrow[step, pl.ds(share, rows - share), :].astype(F32).reshape(n_tm - 1, share, -1).sum(axis=0)
        weights = weights + (residual - product - error * weights) / divisor
        share_weights(step + 1, weights)

    w_ref[...] = weights
    u_ref[...] = weighted(SWEEPS, mixed)

    await_bytes(dall.at[pl.ds(0, (n_obs - 1) * draws)], send_sem.at[0])
    await_bytes(frow.at[pl.ds(share, rows - share)], send_sem.at[1])
    await_bytes(psend.at[pl.ds(share, rows - share)], send_sem.at[2])
    await_bytes(mrow.at[pl.ds(share, rows - share)], send_sem.at[3])
    for step in range(SWEEPS + 1):
        await_bytes(wall.at[step, pl.ds(share, rows - share)], send_sem.at[4 + step])
        await_bytes(gp.at[step, pl.ds(draws, (n_obs - 1) * draws)], send_sem.at[7 + step])
    for step in range(SWEEPS):
        await_bytes(gall.at[step, pl.ds(draws, (n_obs - 1) * draws)], send_sem.at[10 + step])
        await_bytes(ysend.at[step, pl.ds(share, rows - share)], send_sem.at[12 + step])


def body(n_obs, n_tm, footprints, spatial_cov, time_cov, flux_draws, perturbed, obs_error):
    rows, _, cells = footprints.shape
    own_draws = flux_draws.shape[0]
    draws = own_draws * n_obs
    share = rows // n_tm
    any_space = pl.BlockSpec(memory_space=pl.ANY)
    vmem = pl.BlockSpec(memory_space=pltpu.VMEM)
    weights, update = pl.pallas_call(
        functools.partial(kernel, n_obs, n_tm),
        out_shape=(
            jax.ShapeDtypeStruct((share, draws), F32),
            jax.ShapeDtypeStruct((own_draws, cells), F32),
        ),
        in_specs=[any_space, any_space, vmem, any_space, any_space, vmem],
        out_specs=(vmem, vmem),
        scratch_shapes=[
            pltpu.VMEM((rows, cells), BF16),
            pltpu.VMEM((cells, cells), BF16),
            pltpu.VMEM((rows, cells), BF16),
            pltpu.VMEM((rows, cells), BF16),
            pltpu.VMEM((rows, cells), BF16),
            pltpu.VMEM((rows, cells), BF16),
            pltpu.VMEM((draws, cells), BF16),
            pltpu.VMEM((rows, draws), F32),
            pltpu.VMEM((rows, draws), F32),
            pltpu.VMEM((SWEEPS + 1, rows, draws), BF16),
            pltpu.VMEM((draws, rows), BF16),
            pltpu.VMEM((SWEEPS + 1, draws, cells), BF16),
            pltpu.VMEM((SWEEPS + 1, draws, cells), BF16),
            pltpu.VMEM((SWEEPS, draws, cells), BF16),
            pltpu.VMEM((SWEEPS, rows, draws), BF16),
            pltpu.VMEM((SWEEPS, rows, draws), BF16),
            pltpu.VMEM((rows, rows), BF16),
            pltpu.VMEM((rows, rows), BF16),
            pltpu.VMEM((share, draws), F32),
            pltpu.VMEM((share, TILE), F32),
            pltpu.SemaphoreType.DMA((6,)),
            pltpu.SemaphoreType.DMA((14,)),
            pltpu.SemaphoreType.DMA((14,)),
            pltpu.SemaphoreType.DMA((BATCHES,)),
        ],
        compiler_params=pltpu.CompilerParams(
            collective_id=0, has_side_effects=True, vmem_limit_bytes=56 * 1024 * 1024
        ),
    )(
        footprints[:, 0, :], spatial_cov, time_cov, flux_draws[:, 0, :],
        perturbed, obs_error[None, :],
    )
    return weights, update[:, None, :]


def solution(mesh):
    n_obs, n_tm = mesh.shape["obs"], mesh.shape["tm"]
    in_specs = (P("obs", "tm", None), P(), P(), P("obs", "tm", None), P("obs", None), P("obs"))
    out_specs = (P(("obs", "tm"), None), P("obs", "tm", None))
    return jax.shard_map(
        functools.partial(body, n_obs, n_tm), mesh=mesh, in_specs=in_specs, out_specs=out_specs, check_vma=False
    )
```

time: 677 us -> 198 us (0.29)
  waiting for transfers between devices: 358 us -> 0 us
  Pallas kernels: 0 us -> 194 us
  blocking collectives: 166 us -> 0 us
  matrix products: 56.7 us -> 0 us
  local copies, waits for them, and re-layouts: 44.6 us -> 3.3 us
  other arithmetic: 23.8 us -> 0 us
  between operations: 13.9 us -> 0.64 us
  starting transfers between devices: 12.2 us -> 0 us
    psum x1 -> x0, waiting for transfers between devices: 211 us -> none  [body(): lax.psum(jnp.concatenate([contract_last(mixed, all_footprints), contract_...]
    pallas_call x0 -> x1, Pallas kernels: none -> 194 us  [body(): pl.pallas_call(functools.partial(kernel, n_obs, n_tm), out_shape=(jax.Sha...]
    all_to_all x1 -> x0, blocking collectives: 166 us -> none  [body(): lax.all_to_all(spread[:, None, :], 'tm', split_axis=2, concat_axis=1, til...]
    all_gather x3 -> x0, waiting for transfers between devices: 95.2 us -> none  [the longest x2 95.2 us: body(): gathered = lax.all_gather(weights, 'obs', axis=0, tiled=True)]
    dot_general x7 -> x0, matrix products: 56.7 us -> none  [the longest x2 22.5 us: body(): product = jnp.dot(covariance, gathered, precision=lax.Precision.HIGHEST)]
    all_to_all x3 -> x0, waiting for transfers between devices: 51.5 us -> none  [the longest x1 26.4 us: summed_on_arrival(): lax.all_to_all(parts, axis, split_axis=0, concat_axis=0, tiled=True)]
    unnamed x1 -> x0, other arithmetic: 14.1 us -> none
    all_to_all x3 -> x0, starting transfers between devices: 11.8 us -> none  [the longest x1 4.66 us: body(): lax.all_to_all(mixing, 'tm', split_axis=1, concat_axis=2, tiled=True)]
  transfers between devices with their start and end apart: 7 -> 0, of which waited for: 5 -> 0; matrix products, arithmetic and copies ran while one was open for 10% -> 0% of each run, Pallas kernels for 0% -> 0%
where the time goes in v1:
time: 198 us
  Pallas kernels  194 us (98%)
  local copies, waits for them, and re-layouts  3.3 us (2%)
    pallas_call x1, Pallas kernels, body(): pl.pallas_call(functools.partial(kernel, n_obs, n_tm), out_shape=(jax.Sha...  194 us

profile of v1, /device:TPU:1, one launch (start us, length us, event | category | flops | bytes accessed | tf_op | source)
XLA Modules:
  0.0 198.1 jit_solution(16007742874088311719)
XLA Ops:
  0.6 194.2 %shard_map.77 = (f32[32,256]{1,0:T(8,128)}, f32[32,2048]{1,0:T(8,128)}) custom-call(bf16[512,2048]{1,0:T(8,128)(2,1)} %bitcast.4, bf16[2048,2048]{1,0:T(8,128)(2,1)} %s_ref.1, f32[16,16]{1,0:T(8,128)} %t_ref.1, bf16[32,2048]{1,0:T(8,128)(2,1)} %bitcast.6, f32[512,256]{1,0:T(8,128)} %p_ref.1, f32[1,512]{1,0:T(1,128)} %bitcast.7), custom_call_target="tpu_custom_call" | custom-call | tf_op jit(solution)/shard_map/pallas_call | solution.py:247
  194.9 1.9 copy.8
  196.8 1.4 copy.10

commit v2 on v1

v2 whole, which is shorter than its diff:
```python
import functools

import jax
import jax.numpy as jnp
from jax import lax
from jax.experimental import pallas as pl
from jax.experimental.pallas import tpu as pltpu
from jax.sharding import PartitionSpec as P

SWEEPS = 2
MESH = pl.DeviceIdType.MESH
BF16 = jnp.bfloat16
F32 = jnp.float32
TILE = 512
PIECES = 2
HALVES = 2
DRAWS_Z, DRAWS_Y, FOOT, PRED, MIXED = range(5)
WEIGHTS = 5
PARTS = WEIGHTS + (SWEEPS + 1) * HALVES
PARTS_Z = PARTS + (SWEEPS + 1) * HALVES
SUMS_Z = PARTS_Z + (SWEEPS + 1) * HALVES
SUMS = SUMS_Z + SWEEPS * HALVES
PRODUCTS = SUMS + SWEEPS * HALVES
EXCHANGES = PRODUCTS + SWEEPS * HALVES
TM_STEPS = (
    (0, 0, 0), (1, 0, 0), (3, 0, 0), (0, 1, 0), (2, 0, 0), (1, 1, 0), (3, 1, 0), (0, 1, 1),
    (2, 1, 0), (1, 0, 1), (3, 0, 1), (2, 0, 1), (1, 1, 1), (3, 1, 1), (2, 1, 1), (0, 0, 1),
)
OBS_STEPS = ((0, 0), (1, 0), (3, 0), (0, 1), (2, 0), (1, 1), (3, 1), (2, 1))


def dot_nt(left, right):
    return lax.dot_general(left, right, (((1,), (1,)), ((), ())), preferred_element_type=F32)


def dot_nn(left, right):
    return jnp.dot(left, right, preferred_element_type=F32)


def rows_at(start, size):
    return pl.ds(pl.multiple_of(start, size), size)


def kernel(
    n_obs, n_tm,
    f_ref, s_ref, t_ref, d_ref, p_ref, e_ref,
    w_ref, u_ref,
    f_v, s_v, frow, mrow, mixed, dall, psend, prow,
    wall, wt, gp, grs, gz_send, gz, gall, ysend, yrow, mixer, pert, dacc,
    local_sem, send_sem, recv_sem, frecv_sem,
):
    o = lax.axis_index("obs")
    t = lax.axis_index("tm")
    rows, cells = f_ref.shape
    share = rows // n_tm
    draws = d_ref.shape[0]
    part = share // PIECES
    piece_rows = rows // PIECES
    half = draws * n_obs // HALVES
    owned = half // n_obs
    x, z_far, core = t // 4, lax.rem(t // 2, 2), lax.rem(t, 2)
    z_near, y = o // 4, lax.rem(o, 4)

    def tm_at(dx, dz, dc):
        return lax.rem(x + dx, 4) * 4 + lax.rem(z_far + dz, 2) * 2 + lax.rem(core + dc, 2)

    def obs_at(dy, dz):
        return lax.rem(z_near + dz, 2) * 4 + lax.rem(y + dy, 4)

    tm_to = [tm_at(*step) for step in TM_STEPS]
    tm_from = [tm_at(4 - dx, dz, dc) for dx, dz, dc in TM_STEPS]
    obs_to = [obs_at(*step) for step in OBS_STEPS]
    own_share = rows_at(t * share, share)

    unsent = []

    def send(src, dst, phase, axis, peer, recv=None):
        pltpu.make_async_remote_copy(
            src_ref=src, dst_ref=dst, send_sem=send_sem.at[phase],
            recv_sem=recv_sem.at[phase] if recv is None else recv,
            device_id={axis: peer}, device_id_type=MESH,
        ).start()

    def await_bytes(region, sem):
        pltpu.make_async_copy(region, region, sem).wait()

    def sent_later(region, phase):
        unsent.append((region, send_sem.at[phase]))

    load_s = pltpu.make_async_copy(s_ref, s_v, local_sem.at[0])
    load_f = pltpu.make_async_copy(f_ref, f_v, local_sem.at[1])
    load_p = pltpu.make_async_copy(p_ref.at[own_share], pert, local_sem.at[2])
    own_f = [
        pltpu.make_async_copy(
            f_ref.at[rows_at(t * share + piece * part, part)],
            frow.at[pl.ds(piece * piece_rows, part)], local_sem.at[5 + piece],
        )
        for piece in range(PIECES)
    ]

    def half_rows(h, owner):
        return rows_at(h * half + owner * owned, owned)

    own_d = [
        pltpu.make_async_copy(d_ref.at[pl.ds(h * owned, owned)], dall.at[half_rows(h, o)], local_sem.at[(4, 9)[h]])
        for h in range(HALVES)
    ]

    barrier = pltpu.get_barrier_semaphore()
    for peer in tm_to[1:]:
        pl.semaphore_signal(barrier, inc=1, device_id={"tm": peer}, device_id_type=MESH)
    for peer in obs_to[1:]:
        pl.semaphore_signal(barrier, inc=1, device_id={"obs": peer}, device_id_type=MESH)

    load_f.start()
    for copy in own_f:
        copy.start()
    for copy in own_d:
        copy.start()
    load_p.start()
    load_s.start()
    pl.semaphore_wait(barrier, n_tm - 1 + n_obs - 1)

    z_peer = obs_at(0, 1)
    for h in range(HALVES):
        send(d_ref.at[pl.ds(h * owned, owned)], dall.at[half_rows(h, o)], DRAWS_Z, "obs", z_peer)
    sent_later(dall.at[pl.ds(0, draws)], DRAWS_Z)
    for piece in range(PIECES):
        for r in range(1, n_tm):
            send(
                f_ref.at[rows_at(tm_to[r] * share + piece * part, part)],
                frow.at[pl.ds(piece * piece_rows + r * part, part)],
                FOOT, "tm", tm_to[r], frecv_sem.at[piece],
            )
    sent_later(frow.at[pl.ds(share, rows - share)], FOOT)
    for dy in range(1, 4):
        for h in range(HALVES):
            send(d_ref.at[pl.ds(h * owned, owned)], dall.at[half_rows(h, o)], DRAWS_Y, "obs", obs_at(dy, 0))
    await_bytes(dall.at[pl.ds(0, draws)], recv_sem.at[DRAWS_Z])
    for dy in range(1, 4):
        for h in range(HALVES):
            here = dall.at[half_rows(h, z_peer)]
            send(here, here, DRAWS_Y, "obs", obs_at(dy, 0))
    sent_later(dall.at[pl.ds(0, 6 * draws)], DRAWS_Y)

    def periods(shape, dim):
        slot = lax.broadcasted_iota(jnp.int32, shape, dim) // part
        period = jnp.zeros(shape, jnp.int32)
        for r in range(n_tm):
            period = jnp.where(slot == r, tm_from[r], period)
        return period

    pick = (periods((piece_rows, n_tm), 0) == lax.broadcasted_iota(jnp.int32, (piece_rows, n_tm), 1)).astype(F32)
    pick_t = (periods((n_tm, piece_rows), 1) == lax.broadcasted_iota(jnp.int32, (n_tm, piece_rows), 0)).astype(F32)
    picked = jnp.dot(t_ref[...], pick_t, precision=lax.Precision.HIGHEST, preferred_element_type=F32)
    full = jnp.dot(pick, picked, precision=lax.Precision.HIGHEST, preferred_element_type=F32)
    row_in = lax.rem(lax.broadcasted_iota(jnp.int32, (piece_rows, piece_rows), 0), part)
    col_in = lax.rem(lax.broadcasted_iota(jnp.int32, (piece_rows, piece_rows), 1), part)
    full = jnp.where(row_in == col_in, full, 0.0)
    high = full.astype(BF16)
    mixer[pl.ds(0, piece_rows), :] = high
    mixer[pl.ds(piece_rows, piece_rows), :] = (full - high.astype(F32)).astype(BF16)
    dacc[...] = jnp.zeros_like(dacc)

    load_f.wait()
    for copy in own_d:
        copy.wait()
    await_bytes(dall.at[pl.ds(0, 6 * draws)], recv_sem.at[DRAWS_Y])
    psend[...] = dot_nt(f_v[...], dall[...])
    for r in range(1, n_tm):
        send(psend.at[rows_at(tm_to[r] * share, share)], prow.at[pl.ds(r * share, share)], PRED, "tm", tm_to[r])
    sent_later(psend.at[pl.ds(share, rows - share)], PRED)

    def send_mixed(piece):
        pltpu.make_async_copy(
            mrow.at[pl.ds(piece * piece_rows, part)],
            mixed.at[rows_at(t * share + piece * part, part)], local_sem.at[7 + piece],
        ).start()
        for r in range(1, n_tm):
            send(
                mrow.at[pl.ds(piece * piece_rows + r * part, part)],
                mixed.at[rows_at(t * share + piece * part, part)], MIXED, "tm", tm_from[r],
            )

    load_s.wait()
    for piece in range(PIECES):
        own_f[piece].wait()
        await_bytes(frow.at[pl.ds(piece * piece_rows + part, piece_rows - part)], frecv_sem.at[piece])
        here = pl.ds(piece * piece_rows, piece_rows)

        @pl.loop(0, cells // TILE)
        def _(c):
            cols = pl.ds(pl.multiple_of(c * TILE, TILE), TILE)
            block = dot_nn(frow[here, :], s_v[:, cols]).astype(BF16)
            both = dot_nn(mixer[...], block)
            out = (both[:piece_rows] + both[piece_rows:]).astype(BF16)
            mrow[here, cols] = out
            product = out.astype(F32) * frow[here, cols].astype(F32)
            dacc[pl.ds(piece * part, part), :] += product.reshape(n_tm, part, TILE).sum(axis=0)

        if piece < PIECES - 1:
            send_mixed(piece)

    load_p.wait()
    await_bytes(prow.at[pl.ds(share, rows - share)], recv_sem.at[PRED])
    predicted = psend[own_share, :]
    predicted += prow[pl.ds(share, rows - share), :].reshape(n_tm - 1, share, -1).sum(axis=0)
    at_row = lax.broadcasted_iota(jnp.int32, (share, rows), 0) + t * share
    at_col = lax.broadcasted_iota(jnp.int32, (share, rows), 1)
    error = jnp.where(at_row == at_col, jnp.broadcast_to(e_ref[...], (share, rows)), 0.0).sum(axis=1, keepdims=True)
    divisor = dacc[...].sum(axis=1, keepdims=True) + error
    column = lax.broadcasted_iota(jnp.int32, (n_obs * draws, n_obs * draws), 1)
    in_half = lax.rem(column, half)
    draw = in_half // owned * draws + column // half * owned + lax.rem(column, owned)
    order = (lax.broadcasted_iota(jnp.int32, column.shape, 0) == draw).astype(F32)
    ordered = jnp.dot(pert[...], order, precision=lax.Precision.HIGHEST, preferred_element_type=F32)
    whole = ordered - predicted
    residual = [whole[:, h * half:(h + 1) * half] for h in range(HALVES)]

    def send_weights(step, h, weights):
        wall[step, h, own_share, :] = weights.astype(BF16)
        here = wall.at[step, h, own_share]
        phase = WEIGHTS + step * HALVES + h
        for r in range(1, n_tm):
            send(here, here, phase, "tm", tm_to[r])
        sent_later(wall.at[step, h, pl.ds(share, rows - share)], phase)

    def receive_weights(step, h):
        await_bytes(wall.at[step, h, pl.ds(share, rows - share)], recv_sem.at[WEIGHTS + step * HALVES + h])
        wt[pl.ds(h * half, half), :] = wall[step, h].T

    def back_project(step, h):
        receive_weights(step, h)

        source = f_v if step < SWEEPS else mixed
        gp[step, h] = dot_nn(wt[pl.ds(h * half, half), :], source[...]).astype(BF16)
        phase = PARTS + step * HALVES + h
        for dz in range(2):
            for dy in range(1, 4):
                send(
                    gp.at[step, h, rows_at(obs_at(dy, 1 - dz) * owned, owned)],
                    grs.at[step, h, pl.ds(((1 - dz) * 3 + dy - 1) * owned, owned)], phase, "obs", obs_at(dy, 0),
                )
        sent_later(grs.at[step, h], phase)

    def line_sum(step, h, dz):
        total = gp[step, h, rows_at(obs_at(0, dz) * owned, owned), :].astype(F32)
        for dy in range(3):
            total += grs[step, h, pl.ds((dz * 3 + dy) * owned, owned), :].astype(F32)
        return total

    def pass_parts(step, h):
        await_bytes(grs.at[step, h], recv_sem.at[PARTS + step * HALVES + h])
        gz_send[step, h] = line_sum(step, h, 1).astype(BF16)
        phase = PARTS_Z + step * HALVES + h
        send(gz_send.at[step, h], gz.at[step, h], phase, "obs", z_peer)
        sent_later(gz_send.at[step, h], phase)

    def received_sum(step, h):
        await_bytes(gz.at[step, h], recv_sem.at[PARTS_Z + step * HALVES + h])
        return line_sum(step, h, 0) + gz[step, h].astype(F32)

    def sum_parts(step, h):
        here = gall.at[step, h, rows_at(o * owned, owned)]
        here[...] = received_sum(step, h).astype(BF16)
        send(here, here, SUMS_Z + step * HALVES + h, "obs", z_peer)
        sent_later(here, SUMS_Z + step * HALVES + h)
        for dy in range(1, 4):
            send(here, here, SUMS + step * HALVES + h, "obs", obs_at(dy, 0))

    def pass_sums(step, h):
        here = gall.at[step, h, rows_at(z_peer * owned, owned)]
        await_bytes(here, recv_sem.at[SUMS_Z + step * HALVES + h])
        for dy in range(1, 4):
            send(here, here, SUMS + step * HALVES + h, "obs", obs_at(dy, 0))
        sent_later(grs.at[step, h], SUMS + step * HALVES + h)

    def exchange(step):
        pass_parts(step, 0)
        pass_parts(step, 1)
        sum_parts(step, 0)
        pass_sums(step, 0)
        sum_parts(step, 1)
        pass_sums(step, 1)

    def project(step, h):
        await_bytes(grs.at[step, h], recv_sem.at[SUMS + step * HALVES + h])
        ysend[step, h] = dot_nt(mixed[...], gall[step, h]).astype(BF16)
        phase = PRODUCTS + step * HALVES + h
        for r in range(1, n_tm):
            send(
                ysend.at[step, h, rows_at(tm_to[r] * share, share)],
                yrow.at[step, h, pl.ds(r * share, share)], phase, "tm", tm_to[r],
            )
        sent_later(ysend.at[step, h, pl.ds(share, rows - share)], phase)

    def correct(step, h):
        await_bytes(yrow.at[step, h, pl.ds(share, rows - share)], recv_sem.at[PRODUCTS + step * HALVES + h])
        product = ysend[step, h, own_share, :].astype(F32)
        received = yrow[step, h, pl.ds(share, rows - share), :].astype(F32)
        product += received.reshape(n_tm - 1, share, half).sum(axis=0)
        weights[h] = weights[h] + (residual[h] - product - error * weights[h]) / divisor
        send_weights(step + 1, h, weights[h])

    weights = [residual[h] / divisor for h in range(HALVES)]
    for h in range(HALVES):
        send_weights(0, h, weights[h])
    send_mixed(PIECES - 1)
    sent_later(mrow.at[pl.ds(share, rows - share)], MIXED)

    back_project(0, 0)
    back_project(0, 1)
    exchange(0)
    for piece in range(PIECES):
        pltpu.make_async_copy(
            mrow.at[pl.ds(0, part)], mixed.at[pl.ds(0, part)], local_sem.at[7 + piece]
        ).wait()
    await_bytes(mixed.at[pl.ds(share, rows - share)], recv_sem.at[MIXED])
    for step in range(SWEEPS):
        project(step, 0)
        correct(step, 0)
        project(step, 1)
        back_project(step + 1, 0)
        correct(step, 1)
        back_project(step + 1, 1)
        if step < SWEEPS - 1:
            exchange(step + 1)

    for h in range(HALVES):
        pass_parts(SWEEPS, h)
    last = jnp.concatenate(weights, axis=1)
    w_ref[...] = lax.dot_general(
        last, order, (((1,), (1,)), ((), ())), precision=lax.Precision.HIGHEST, preferred_element_type=F32
    )
    for h in range(HALVES):
        u_ref[pl.ds(h * owned, owned), :] = received_sum(SWEEPS, h)

    for region, sem in unsent:
        await_bytes(region, sem)


def body(n_obs, n_tm, footprints, spatial_cov, time_cov, flux_draws, perturbed, obs_error):
    rows, _, cells = footprints.shape
    own_draws = flux_draws.shape[0]
    draws = own_draws * n_obs
    share = rows // n_tm
    half = draws // HALVES
    any_space = pl.BlockSpec(memory_space=pl.ANY)
    vmem = pl.BlockSpec(memory_space=pltpu.VMEM)
    weights, update = pl.pallas_call(
        functools.partial(kernel, n_obs, n_tm),
        out_shape=(
            jax.ShapeDtypeStruct((share, draws), F32),
            jax.ShapeDtypeStruct((own_draws, cells), F32),
        ),
        in_specs=[any_space, any_space, vmem, any_space, any_space, vmem],
        out_specs=(vmem, vmem),
        scratch_shapes=[
            pltpu.VMEM((rows, cells), BF16),
            pltpu.VMEM((cells, cells), BF16),
            pltpu.VMEM((rows, cells), BF16),
            pltpu.VMEM((rows, cells), BF16),
            pltpu.VMEM((rows, cells), BF16),
            pltpu.VMEM((draws, cells), BF16),
            pltpu.VMEM((rows, draws), F32),
            pltpu.VMEM((rows, draws), F32),
            pltpu.VMEM((SWEEPS + 1, HALVES, rows, half), BF16),
            pltpu.VMEM((draws, rows), BF16),
            pltpu.VMEM((SWEEPS + 1, HALVES, half, cells), BF16),
            pltpu.VMEM((SWEEPS + 1, HALVES, 6 * half // n_obs, cells), BF16),
            pltpu.VMEM((SWEEPS + 1, HALVES, half // n_obs, cells), BF16),
            pltpu.VMEM((SWEEPS + 1, HALVES, half // n_obs, cells), BF16),
            pltpu.VMEM((SWEEPS, HALVES, half, cells), BF16),
            pltpu.VMEM((SWEEPS, HALVES, rows, half), BF16),
            pltpu.VMEM((SWEEPS, HALVES, rows, half), BF16),
            pltpu.VMEM((2 * rows // PIECES, rows // PIECES), BF16),
            pltpu.VMEM((share, draws), F32),
            pltpu.VMEM((share, TILE), F32),
            pltpu.SemaphoreType.DMA((10,)),
            pltpu.SemaphoreType.DMA((EXCHANGES,)),
            pltpu.SemaphoreType.DMA((EXCHANGES,)),
            pltpu.SemaphoreType.DMA((PIECES,)),
        ],
        compiler_params=pltpu.CompilerParams(
            collective_id=0, has_side_effects=True, vmem_limit_bytes=56 * 1024 * 1024
        ),
    )(
        footprints[:, 0, :], spatial_cov, time_cov, flux_draws[:, 0, :],
        perturbed, obs_error[None, :],
    )
    return weights, update[:, None, :]


def solution(mesh):
    n_obs, n_tm = mesh.shape["obs"], mesh.shape["tm"]
    in_specs = (P("obs", "tm", None), P(), P(), P("obs", "tm", None), P("obs", None), P("obs"))
    out_specs = (P(("obs", "tm"), None), P("obs", "tm", None))
    return jax.shard_map(
        functools.partial(body, n_obs, n_tm), mesh=mesh, in_specs=in_specs, out_specs=out_specs, check_vma=False
    )
```

time: 198 us -> 160 us (0.81)
  Pallas kernels: 194 us -> 156 us
    pallas_call x1, Pallas kernels: 194 us -> 156 us  [body(): pl.pallas_call(functools.partial(kernel, n_obs, n_tm), out_shape=(jax.Sha...]
where the time goes in v2:
time: 160 us
  Pallas kernels  156 us (98%)
  local copies, waits for them, and re-layouts  3.3 us (2%)
    pallas_call x1, Pallas kernels, body(): pl.pallas_call(functools.partial(kernel, n_obs, n_tm), out_shape=(jax.Sha...  156 us
    unnamed x2, local copies, waits for them, and re-layouts  3.3 us

profile of v2, /device:TPU:1, one launch (start us, length us, event | category | flops | bytes accessed | tf_op | source)
XLA Modules:
  0.0 159.8 jit_solution(13054516170163686585)
XLA Ops:
  0.6 155.8 %shard_map.77 = (f32[32,256]{1,0:T(8,128)}, f32[32,2048]{1,0:T(8,128)}) custom-call(bf16[512,2048]{1,0:T(8,128)(2,1)} %bitcast.4, bf16[2048,2048]{1,0:T(8,128)(2,1)} %s_ref.1, f32[16,16]{1,0:T(8,128)} %t_ref.1, bf16[32,2048]{1,0:T(8,128)(2,1)} %bitcast.6, f32[512,256]{1,0:T(8,128)} %p_ref.1, f32[1,512]{1,0:T(1,128)} %bitcast.7), custom_call_target="tpu_custom_call" | custom-call | tf_op jit(solution)/shard_map/pallas_call | solution.py:350
  156.5 1.9 %copy.8 = f32[32,1,2048]{2,1,0:T(1,128)} copy(f32[32,1,2048]{2,0,1:T(8,128)} %bitcast.5) | data formatting | bytes 524288
  158.4 1.4 copy.10

commit v3 on v2

--- a/solution.py
+++ b/solution.py
@@ -14,6 +14,7 @@
 TILE = 512
 PIECES = 2
 HALVES = 2
+STAGED = (True, False, False)
 DRAWS_Z, DRAWS_Y, FOOT, PRED, MIXED = range(5)
 WEIGHTS = 5
 PARTS = WEIGHTS + (SWEEPS + 1) * HALVES
@@ -125,13 +126,15 @@
     for h in range(HALVES):
         send(d_ref.at[pl.ds(h * owned, owned)], dall.at[half_rows(h, o)], DRAWS_Z, "obs", z_peer)
     sent_later(dall.at[pl.ds(0, draws)], DRAWS_Z)
-    for piece in range(PIECES):
+    def send_footprints(piece):
         for r in range(1, n_tm):
             send(
                 f_ref.at[rows_at(tm_to[r] * share + piece * part, part)],
                 frow.at[pl.ds(piece * piece_rows + r * part, part)],
                 FOOT, "tm", tm_to[r], frecv_sem.at[piece],
             )
+
+    send_footprints(0)
     sent_later(frow.at[pl.ds(share, rows - share)], FOOT)
     for dy in range(1, 4):
         for h in range(HALVES):
@@ -142,6 +145,17 @@
             here = dall.at[half_rows(h, z_peer)]
             send(here, here, DRAWS_Y, "obs", obs_at(dy, 0))
     sent_later(dall.at[pl.ds(0, 6 * draws)], DRAWS_Y)
+
+    load_f.wait()
+    for copy in own_d:
+        copy.wait()
+    await_bytes(dall.at[pl.ds(0, 6 * draws)], recv_sem.at[DRAWS_Y])
+    psend[...] = dot_nt(f_v[...], dall[...])
+    for r in range(1, n_tm):
+        send(psend.at[rows_at(tm_to[r] * share, share)], prow.at[pl.ds(r * share, share)], PRED, "tm", tm_to[r])
+    sent_later(psend.at[pl.ds(share, rows - share)], PRED)
+    for piece in range(1, PIECES):
+        send_footprints(piece)
 
     def periods(shape, dim):
         slot = lax.broadcasted_iota(jnp.int32, shape, dim) // part
@@ -162,15 +176,6 @@
     mixer[pl.ds(piece_rows, piece_rows), :] = (full - high.astype(F32)).astype(BF16)
     dacc[...] = jnp.zeros_like(dacc)
 
-    load_f.wait()
-    for copy in own_d:
-        copy.wait()
-    await_bytes(dall.at[pl.ds(0, 6 * draws)], recv_sem.at[DRAWS_Y])
-    psend[...] = dot_nt(f_v[...], dall[...])
-    for r in range(1, n_tm):
-        send(psend.at[rows_at(tm_to[r] * share, share)], prow.at[pl.ds(r * share, share)], PRED, "tm", tm_to[r])
-    sent_later(psend.at[pl.ds(share, rows - share)], PRED)
-
     def send_mixed(piece):
         pltpu.make_async_copy(
             mrow.at[pl.ds(piece * piece_rows, part)],
@@ -197,9 +202,6 @@
             mrow[here, cols] = out
             product = out.astype(F32) * frow[here, cols].astype(F32)
             dacc[pl.ds(piece * part, part), :] += product.reshape(n_tm, part, TILE).sum(axis=0)
-
-        if piece < PIECES - 1:
-            send_mixed(piece)
 
     load_p.wait()
     await_bytes(prow.at[pl.ds(share, rows - share)], recv_sem.at[PRED])
@@ -229,51 +231,72 @@
         await_bytes(wall.at[step, h, pl.ds(share, rows - share)], recv_sem.at[WEIGHTS + step * HALVES + h])
         wt[pl.ds(h * half, half), :] = wall[step, h].T
 
+    def targets(step):
+        if STAGED[step]:
+            return [(dy, dz) for dz in (1, 0) for dy in (1, 3, 2)]
+        return OBS_STEPS[1:]
+
     def back_project(step, h):
         receive_weights(step, h)
 
         source = f_v if step < SWEEPS else mixed
         gp[step, h] = dot_nn(wt[pl.ds(h * half, half), :], source[...]).astype(BF16)
         phase = PARTS + step * HALVES + h
-        for dz in range(2):
-            for dy in range(1, 4):
-                send(
-                    gp.at[step, h, rows_at(obs_at(dy, 1 - dz) * owned, owned)],
-                    grs.at[step, h, pl.ds(((1 - dz) * 3 + dy - 1) * owned, owned)], phase, "obs", obs_at(dy, 0),
-                )
-        sent_later(grs.at[step, h], phase)
+        for slot, (dy, dz) in enumerate(targets(step)):
+            send(
+                gp.at[step, h, rows_at(obs_at(dy, dz) * owned, owned)],
+                grs.at[step, h, pl.ds(slot * owned, owned)], phase, "obs",
+                obs_at(dy, 0) if STAGED[step] else obs_at(dy, dz),
+            )
+        sent_later(grs.at[step, h, pl.ds(0, len(targets(step)) * owned)], phase)
 
     def line_sum(step, h, dz):
         total = gp[step, h, rows_at(obs_at(0, dz) * owned, owned), :].astype(F32)
-        for dy in range(3):
-            total += grs[step, h, pl.ds((dz * 3 + dy) * owned, owned), :].astype(F32)
+        for slot, target in enumerate(targets(step)):
+            if not STAGED[step] or target[1] == dz:
+                total += grs[step, h, pl.ds(slot * owned, owned), :].astype(F32)
         return total
 
+    def await_parts(step, h):
+        await_bytes(grs.at[step, h, pl.ds(0, len(targets(step)) * owned)], recv_sem.at[PARTS + step * HALVES + h])
+
     def pass_parts(step, h):
-        await_bytes(grs.at[step, h], recv_sem.at[PARTS + step * HALVES + h])
+        if not STAGED[step]:
+            return
+        await_parts(step, h)
         gz_send[step, h] = line_sum(step, h, 1).astype(BF16)
         phase = PARTS_Z + step * HALVES + h
         send(gz_send.at[step, h], gz.at[step, h], phase, "obs", z_peer)
         sent_later(gz_send.at[step, h], phase)
 
     def received_sum(step, h):
+        if not STAGED[step]:
+            await_parts(step, h)
+            return line_sum(step, h, 0)
         await_bytes(gz.at[step, h], recv_sem.at[PARTS_Z + step * HALVES + h])
         return line_sum(step, h, 0) + gz[step, h].astype(F32)
 
     def sum_parts(step, h):
         here = gall.at[step, h, rows_at(o * owned, owned)]
         here[...] = received_sum(step, h).astype(BF16)
-        send(here, here, SUMS_Z + step * HALVES + h, "obs", z_peer)
-        sent_later(here, SUMS_Z + step * HALVES + h)
-        for dy in range(1, 4):
-            send(here, here, SUMS + step * HALVES + h, "obs", obs_at(dy, 0))
+        phase = SUMS + step * HALVES + h
+        if STAGED[step]:
+            send(here, here, SUMS_Z + step * HALVES + h, "obs", z_peer)
+            sent_later(here, SUMS_Z + step * HALVES + h)
+            for dy in (1, 3, 2):
+                send(here, here, phase, "obs", obs_at(dy, 0))
+        else:
+            for peer in obs_to[1:]:
+                send(here, here, phase, "obs", peer)
+        sent_later(grs.at[step, h, pl.ds(0, len(targets(step)) * owned)], phase)
 
     def pass_sums(step, h):
+        if not STAGED[step]:
+            return
         here = gall.at[step, h, rows_at(z_peer * owned, owned)]
         await_bytes(here, recv_sem.at[SUMS_Z + step * HALVES + h])
-        for dy in range(1, 4):
+        for dy in (1, 3, 2):
             send(here, here, SUMS + step * HALVES + h, "obs", obs_at(dy, 0))
-        sent_later(grs.at[step, h], SUMS + step * HALVES + h)
 
     def exchange(step):
         pass_parts(step, 0)
@@ -284,7 +307,7 @@
         pass_sums(step, 1)
 
     def project(step, h):
-        await_bytes(grs.at[step, h], recv_sem.at[SUMS + step * HALVES + h])
+        await_bytes(grs.at[step, h, pl.ds(0, len(targets(step)) * owned)], recv_sem.at[SUMS + step * HALVES + h])
         ysend[step, h] = dot_nt(mixed[...], gall[step, h]).astype(BF16)
         phase = PRODUCTS + step * HALVES + h
         for r in range(1, n_tm):
@@ -305,11 +328,12 @@
     weights = [residual[h] / divisor for h in range(HALVES)]
     for h in range(HALVES):
         send_weights(0, h, weights[h])
-    send_mixed(PIECES - 1)
+    send_mixed(0)
     sent_later(mrow.at[pl.ds(share, rows - share)], MIXED)
 
     back_project(0, 0)
     back_project(0, 1)
+    send_mixed(1)
     exchange(0)
     for piece in range(PIECES):
         pltpu.make_async_copy(
@@ -318,10 +342,10 @@
     await_bytes(mixed.at[pl.ds(share, rows - share)], recv_sem.at[MIXED])
     for step in range(SWEEPS):
         project(step, 0)
+        project(step, 1)
         correct(step, 0)
-        project(step, 1)
+        correct(step, 1)
         back_project(step + 1, 0)
-        correct(step, 1)
         back_project(step + 1, 1)
         if step < SWEEPS - 1:
             exchange(step + 1)
@@ -367,7 +391,7 @@
             pltpu.VMEM((SWEEPS + 1, HALVES, rows, half), BF16),
             pltpu.VMEM((draws, rows), BF16),
             pltpu.VMEM((SWEEPS + 1, HALVES, half, cells), BF16),
-            pltpu.VMEM((SWEEPS + 1, HALVES, 6 * half // n_obs, cells), BF16),
+            pltpu.VMEM((SWEEPS + 1, HALVES, 7 * half // n_obs, cells), BF16),
             pltpu.VMEM((SWEEPS + 1, HALVES, half // n_obs, cells), BF16),
             pltpu.VMEM((SWEEPS + 1, HALVES, half // n_obs, cells), BF16),
             pltpu.VMEM((SWEEPS, HALVES, half, cells), BF16),

time: 160 us -> 151 us (0.944)
  Pallas kernels: 156 us -> 146 us
    pallas_call x1, Pallas kernels: 156 us -> 146 us  [body(): pl.pallas_call(functools.partial(kernel, n_obs, n_tm), out_shape=(jax.Sha...]
where the time goes in v3:
time: 151 us; the launch traced here: 150 us
  Pallas kernels  146 us (97%)
  local copies, waits for them, and re-layouts  3.3 us (2%)
    pallas_call x1, Pallas kernels, body(): pl.pallas_call(functools.partial(kernel, n_obs, n_tm), out_shape=(jax.Sha...  146 us
    unnamed x2, local copies, waits for them, and re-layouts  3.3 us

profile of v3, /device:TPU:1, one launch (start us, length us, event | category | flops | bytes accessed | tf_op | source)
XLA Modules:
  0.0 150.4 jit_solution(4988710382517689592)
XLA Ops:
  0.6 146.4 %shard_map.77 = (f32[32,256]{1,0:T(8,128)}, f32[32,2048]{1,0:T(8,128)}) custom-call(bf16[512,2048]{1,0:T(8,128)(2,1)} %bitcast.4, bf16[2048,2048]{1,0:T(8,128)(2,1)} %s_ref.1, f32[16,16]{1,0:T(8,128)} %t_ref.1, bf16[32,2048]{1,0:T(8,128)(2,1)} %bitcast.6, f32[512,256]{1,0:T(8,128)} %p_ref.1, f32[1,512]{1,0:T(1,128)} %bitcast.7), custom_call_target="tpu_custom_call" | custom-call | tf_op jit(solution)/shard_map/pallas_call | solution.py:374
  147.1 1.9 %copy.8 = f32[32,1,2048]{2,1,0:T(1,128)} copy(f32[32,1,2048]{2,0,1:T(8,128)} %bitcast.5) | data formatting | bytes 524288
  149.0 1.4 copy.10

commit v4 on v3

--- a/solution.py
+++ b/solution.py
@@ -11,7 +11,7 @@
 MESH = pl.DeviceIdType.MESH
 BF16 = jnp.bfloat16
 F32 = jnp.float32
-TILE = 512
+TILE = 1024
 PIECES = 2
 HALVES = 2
 STAGED = (True, False, False)
@@ -357,7 +357,7 @@
         last, order, (((1,), (1,)), ((), ())), precision=lax.Precision.HIGHEST, preferred_element_type=F32
     )
     for h in range(HALVES):
-        u_ref[pl.ds(h * owned, owned), :] = received_sum(SWEEPS, h)
+        u_ref[pl.ds(h * owned, owned), 0, :] = received_sum(SWEEPS, h)
 
     for region, sem in unsent:
         await_bytes(region, sem)
@@ -375,7 +375,7 @@
         functools.partial(kernel, n_obs, n_tm),
         out_shape=(
             jax.ShapeDtypeStruct((share, draws), F32),
-            jax.ShapeDtypeStruct((own_draws, cells), F32),
+            jax.ShapeDtypeStruct((own_draws, 1, cells), F32),
         ),
         in_specs=[any_space, any_space, vmem, any_space, any_space, vmem],
         out_specs=(vmem, vmem),
@@ -412,7 +412,7 @@
         footprints[:, 0, :], spatial_cov, time_cov, flux_draws[:, 0, :],
         perturbed, obs_error[None, :],
     )
-    return weights, update[:, None, :]
+    return weights, update
 
 
 def solution(mesh):

time: 151 us -> 149 us (0.987)
  no operation moved by 1% of the time
where the time goes in v4:
time: 149 us
  Pallas kernels  145 us (97%)
  local copies, waits for them, and re-layouts  3.04 us (2%)
    pallas_call x1, Pallas kernels, body(): pl.pallas_call(functools.partial(kernel, n_obs, n_tm), out_shape=(jax.Sha...  145 us
    unnamed x2, local copies, waits for them, and re-layouts  3.04 us

profile of v4, /device:TPU:1, one launch (start us, length us, event | category | flops | bytes accessed | tf_op | source)
XLA Modules:
  0.0 149.1 jit_solution(13748133474792259778)
XLA Ops:
  0.6 145.4 %shard_map.77 = (f32[32,256]{1,0:T(8,128)}, f32[32,1,2048]{2,1,0:T(1,128)}) custom-call(bf16[512,2048]{1,0:T(8,128)(2,1)} %bitcast.3, bf16[2048,2048]{1,0:T(8,128)(2,1)} %s_ref.1, f32[16,16]{1,0:T(8,128)} %t_ref.1, bf16[32,2048]{1,0:T(8,128)(2,1)} %bitcast.4, f32[512,256]{1,0:T(8,128)} %p_ref.1, f32[1,512]{1,0:T(1,128)} %bitcast.5), custom_call_target="tpu_custom_call" | custom-call | tf_op jit(solution)/shard_map/pallas_call | solution.py:374
  146.1 1.4 copy.10
  147.4 1.7 %copy.11 = f32[32,1,2048]{2,1,0:T(1,128)} copy(f32[32,1,2048]{2,1,0:T(1,128)} %get-tuple-element.5) | data formatting | bytes 524288

commit v5 on v4

--- a/solution.py
+++ b/solution.py
@@ -187,6 +187,15 @@
                 mixed.at[rows_at(t * share + piece * part, part)], MIXED, "tm", tm_from[r],
             )
 
+    load_p.wait()
+    at_row = lax.broadcasted_iota(jnp.int32, (share, rows), 0) + t * share
+    at_col = lax.broadcasted_iota(jnp.int32, (share, rows), 1)
+    error = jnp.where(at_row == at_col, jnp.broadcast_to(e_ref[...], (share, rows)), 0.0).sum(axis=1, keepdims=True)
+    column = lax.broadcasted_iota(jnp.int32, (n_obs * draws, n_obs * draws), 1)
+    in_half = lax.rem(column, half)
+    draw = in_half // owned * draws + column // half * owned + lax.rem(column, owned)
+    order = (lax.broadcasted_iota(jnp.int32, column.shape, 0) == draw).astype(F32)
+    ordered = jnp.dot(pert[...], order, precision=lax.Precision.HIGHEST, preferred_element_type=F32)
     load_s.wait()
     for piece in range(PIECES):
         own_f[piece].wait()
@@ -203,19 +212,10 @@
             product = out.astype(F32) * frow[here, cols].astype(F32)
             dacc[pl.ds(piece * part, part), :] += product.reshape(n_tm, part, TILE).sum(axis=0)
 
-    load_p.wait()
     await_bytes(prow.at[pl.ds(share, rows - share)], recv_sem.at[PRED])
     predicted = psend[own_share, :]
     predicted += prow[pl.ds(share, rows - share), :].reshape(n_tm - 1, share, -1).sum(axis=0)
-    at_row = lax.broadcasted_iota(jnp.int32, (share, rows), 0) + t * share
-    at_col = lax.broadcasted_iota(jnp.int32, (share, rows), 1)
-    error = jnp.where(at_row == at_col, jnp.broadcast_to(e_ref[...], (share, rows)), 0.0).sum(axis=1, keepdims=True)
     divisor = dacc[...].sum(axis=1, keepdims=True) + error
-    column = lax.broadcasted_iota(jnp.int32, (n_obs * draws, n_obs * draws), 1)
-    in_half = lax.rem(column, half)
-    draw = in_half // owned * draws + column // half * owned + lax.rem(column, owned)
-    order = (lax.broadcasted_iota(jnp.int32, column.shape, 0) == draw).astype(F32)
-    ordered = jnp.dot(pert[...], order, precision=lax.Precision.HIGHEST, preferred_element_type=F32)
     whole = ordered - predicted
     residual = [whole[:, h * half:(h + 1) * half] for h in range(HALVES)]
 

time: 149 us -> 149 us (level)
  no operation moved by 1% of the time
where the time goes in v5:
time: 149 us
  Pallas kernels  145 us (97%)
  local copies, waits for them, and re-layouts  3.04 us (2%)
    pallas_call x1, Pallas kernels, body(): pl.pallas_call(functools.partial(kernel, n_obs, n_tm), out_shape=(jax.Sha...  145 us
    unnamed x2, local copies, waits for them, and re-layouts  3.04 us

profile of v5, /device:TPU:1, one launch (start us, length us, event | category | flops | bytes accessed | tf_op | source)
XLA Modules:
  0.0 148.7 jit_solution(10439433772272297274)
XLA Ops:
  0.6 145.0 %shard_map.77 = (f32[32,256]{1,0:T(8,128)}, f32[32,1,2048]{2,1,0:T(1,128)}) custom-call(bf16[512,2048]{1,0:T(8,128)(2,1)} %bitcast.3, bf16[2048,2048]{1,0:T(8,128)(2,1)} %s_ref.1, f32[16,16]{1,0:T(8,128)} %t_ref.1, bf16[32,2048]{1,0:T(8,128)(2,1)} %bitcast.4, f32[512,256]{1,0:T(8,128)} %p_ref.1, f32[1,512]{1,0:T(1,128)} %bitcast.5), custom_call_target="tpu_custom_call" | custom-call | tf_op jit(solution)/shard_map/pallas_call | solution.py:374
  145.6 1.4 copy.10
  147.0 1.7 %copy.11 = f32[32,1,2048]{2,1,0:T(1,128)} copy(f32[32,1,2048]{2,1,0:T(1,128)} %get-tuple-element.5) | data formatting | bytes 524288
